TPU v7x, 512 devices: a whole 4x8x8 slice. The times are simulated.
512 devices in a mesh: pipe: 32 (over z_lo, y, core), tensor: 16 (over z_hi, x).
Axes of the slice: x: 4, y: 8, z: 8 (z_hi: 4, z_lo: 2; z = z_hi * 2 + z_lo), core: 2. Of those that a mesh axis runs over, the one named last changes fastest.
Arguments:
- tokens: bfloat16 [256, 8192], P('pipe', 'tensor'), may hold values from -6 to 6
- gate_weight: bfloat16 [8192, 28672], P('tensor', 'pipe'), may hold values from -0.0625 to 0.0625
- upward_weight: bfloat16 [8192, 28672], P('tensor', 'pipe'), may hold values from -0.0625 to 0.0625
- down_weight: bfloat16 [28672, 8192], P('pipe', 'tensor'), may hold values from -0.03125 to 0.03125
- adapter_first_factors: bfloat16 [2, 8192, 64], P(None, 'tensor'), may hold values from -0.0625 to 0.0625
- adapter_second_factors: bfloat16 [2, 64, 28672], P(None, None, 'pipe'), may hold values from -0.75 to 0.75
- adapter_of_block: int32 [2], replicated, may hold values from 0 to 1, each once
- cotangent: bfloat16 [256, 8192], P('pipe', 'tensor'), may hold values from -6 to 6
Outputs:
- mixed: bfloat16 [256, 8192], P('pipe', 'tensor')
- grad_tokens: bfloat16 [256, 8192], P('pipe', 'tensor')
- grad_a: float32 [2, 8192, 64], P(None, 'tensor')
- grad_b: float32 [2, 64, 28672], P(None, None, 'pipe')
Inputs may be any that keep to these rules, and one draw needn't show every extreme that they name: `adapter_of_block`: each of the 2 adapters is named by exactly one block.
All inputs are finite; a program needn't handle non-finite values.
Results may differ from a plain program's by a relative error of at most 0.0052.
Values may be sent and summed in bfloat16 or wider, within the bound.
No kernel may reach another device: no remote copies, remote signals or barrier semaphores. Data moves between devices by JAX's collectives and lax.ppermute only.
A program may use at most 64 MiB of HBM per device.

v0:
```python
import jax
import jax.numpy as jnp
from jax import lax
from jax.sharding import PartitionSpec as P

BLOCK = 128
adapter_scale = 0.5


def adapter_mask(first_row, row_count, adapter_of_block, rank_columns):
    row_index = first_row + jnp.arange(row_count, dtype=jnp.int32)
    owner = row_index // BLOCK
    block_index = jnp.arange(adapter_of_block.shape[0], dtype=jnp.int32)
    chosen = jnp.sum(
        jnp.where(owner[:, None] == block_index[None, :], adapter_of_block[None, :], 0), axis=1
    )
    columns = jnp.arange(adapter_of_block.shape[0] * rank_columns, dtype=jnp.int32) // rank_columns
    return (columns[None, :] == chosen[:, None]).astype(jnp.float32)


def trailing_product(left, right):
    return lax.dot_general(
        left, right, (((1,), (1,)), ((), ())), preferred_element_type=jnp.float32
    )


def leading_product(left, right):
    return lax.dot_general(
        left, right, (((0,), (0,)), ((), ())), preferred_element_type=jnp.float32
    )


def on_device(
    tokens,
    gate_weight,
    upward_weight,
    down_weight,
    adapter_first_factors,
    adapter_second_factors,
    adapter_of_block,
    cotangent,
):
    adapter_total, width_shard, rank_columns = adapter_first_factors.shape
    hidden_shard = gate_weight.shape[1]
    first_factor_rows = jnp.transpose(adapter_first_factors, (1, 0, 2)).reshape(
        width_shard, adapter_total * rank_columns
    )
    second_factor_rows = adapter_second_factors.reshape(adapter_total * rank_columns, hidden_shard)
    pipe_rows = tokens.shape[0]
    all_rows = pipe_rows * lax.axis_size("pipe")
    tensor_rows = all_rows // lax.axis_size("tensor")
    token_rows = lax.all_gather(tokens, "pipe", axis=0, tiled=True)
    piece = token_rows
    parts = lax.psum_scatter(
        jnp.concatenate(
            [
                jnp.dot(piece, gate_weight, preferred_element_type=jnp.float32),
                jnp.dot(piece, upward_weight, preferred_element_type=jnp.float32),
                jnp.dot(piece, first_factor_rows, preferred_element_type=jnp.float32),
            ],
            axis=1,
        ),
        "tensor",
        scatter_dimension=0,
        tiled=True,
    )
    first_row = lax.axis_index("tensor") * tensor_rows
    adapter_select_mask = adapter_mask(first_row, parts.shape[0], adapter_of_block, rank_columns)
    gate = parts[:, :hidden_shard]
    upward_frozen_output = parts[:, hidden_shard : 2 * hidden_shard]
    reduced_activation = (parts[:, 2 * hidden_shard :] * adapter_select_mask).astype(jnp.bfloat16)
    upward_output = upward_frozen_output + adapter_scale * jnp.dot(
        reduced_activation, second_factor_rows, preferred_element_type=jnp.float32
    )
    sig = jax.nn.sigmoid(gate)
    act = gate * sig
    hidden = (act * upward_output).astype(jnp.bfloat16)
    hidden_all = lax.all_gather(hidden, "tensor", axis=0, tiled=True)
    piece = hidden_all
    mixed = lax.psum_scatter(
        jnp.dot(piece, down_weight, preferred_element_type=jnp.float32),
        "pipe",
        scatter_dimension=0,
        tiled=True,
    ).astype(jnp.bfloat16)
    adjoint_rows = lax.all_gather(cotangent, "pipe", axis=0, tiled=True)
    piece = adjoint_rows
    grad_hidden = lax.psum_scatter(
        trailing_product(piece, down_weight), "tensor", scatter_dimension=0, tiled=True
    )
    upward_gradient = (grad_hidden * act).astype(jnp.bfloat16)
    grad_gate = (grad_hidden * upward_output * sig * (1.0 + gate * (1.0 - sig))).astype(
        jnp.bfloat16
    )
    second_factor_term = adapter_scale * leading_product(reduced_activation, upward_gradient)
    second_factor_gradient = lax.psum(second_factor_term, "tensor")
    reduced_gradient = (
        adapter_scale * trailing_product(upward_gradient, second_factor_rows) * adapter_select_mask
    )
    low_summed = lax.psum(reduced_gradient, "pipe")
    low_all = lax.all_gather(low_summed, "tensor", axis=0, tiled=True)
    low_back = low_all.astype(jnp.bfloat16)
    stacked = jnp.concatenate([grad_gate, upward_gradient], axis=1)
    stacked_all = lax.all_gather(stacked, "tensor", axis=0, tiled=True)
    piece = stacked_all
    back_sum = lax.psum_scatter(
        trailing_product(piece[:, :hidden_shard], gate_weight)
        + trailing_product(piece[:, hidden_shard:], upward_weight),
        "pipe",
        scatter_dimension=0,
        tiled=True,
    )
    own_low = lax.dynamic_slice_in_dim(low_back, lax.axis_index("pipe") * pipe_rows, pipe_rows, 0)
    grad_tokens = (back_sum + trailing_product(own_low, first_factor_rows)).astype(jnp.bfloat16)
    grad_a_flat = leading_product(token_rows, low_back)
    grad_a = jnp.transpose(grad_a_flat.reshape(width_shard, adapter_total, rank_columns), (1, 0, 2))
    grad_b = second_factor_gradient.reshape(adapter_total, rank_columns, hidden_shard)
    return (mixed, grad_tokens, grad_a, grad_b)


def solution(mesh):
    in_specs = (
        P("pipe", "tensor"),
        P("tensor", "pipe"),
        P("tensor", "pipe"),
        P("pipe", "tensor"),
        P(None, "tensor", None),
        P(None, None, "pipe"),
        P(),
        P("pipe", "tensor"),
    )
    out_specs = (
        P("pipe", "tensor"),
        P("pipe", "tensor"),
        P(None, "tensor", None),
        P(None, None, "pipe"),
    )
    return jax.shard_map(
        on_device, mesh=mesh, in_specs=in_specs, out_specs=out_specs, check_vma=False
    )
```

profile of v0, /device:TPU:2, one launch (start us, length us, event | category | flops | bytes accessed | tf_op | source)
XLA Modules:
  0.0 687.5 jit_solution(7951810947184697650)
XLA Ops:
  7.2 0.0 copy-start
  7.2 0.0 copy-start.4
  7.2 0.0 copy-start.3
  7.2 0.0 reduce-scatter.9.cloned.1.call-start
  7.2 36.7 %all_gather.17 = bf16[256,512]{1,0:T(8,128)(2,1)S(1)} all-gather(bf16[8,512]{1,0:T(8,128)(2,1)} %param.15), channel_id=1, replica_groups=mesh['pipe'=32,'tensor'=16] {'pipe'}, dimensions={0}, use_global_device_ids=true | all-gather | bytes 270336 | tf_op jit(solution)/shard_map/all_gather | solution.py:86
  44.0 0.0 copy-done
  44.0 0.0 copy-start.1
  44.0 1.4 fusion.17
  45.4 0.0 copy-start.2
  45.4 0.0 reduce-scatter.9.cloned.1.call-update
  45.4 0.0 reduce-scatter.5.cloned.1.call-start
  45.5 0.0 copy-done.4
  45.5 31.6 %all_gather.15 = bf16[256,512]{1,0:T(8,128)(2,1)S(1)} all-gather(bf16[8,512]{1,0:T(8,128)(2,1)S(1)} %copy-done.4), channel_id=1, replica_groups=mesh['pipe'=32,'tensor'=16] {'pipe'}, dimensions={0}, use_global_device_ids=true | all-gather | bytes 270336 | tf_op jit(solution)/shard_map/all_gather | solution.py:52
  77.1 0.0 copy-done.3
  77.1 0.2 fusion.15
  77.3 0.0 copy-done.1
  77.3 0.4 fusion.13
  77.8 0.0 copy-done.2
  77.8 0.4 fusion.14
  78.2 1.4 pad_maximum_fusion
  79.6 0.0 copy-start.6
  79.6 0.0 copy-start.5
  79.6 0.0 reduce-scatter.5.cloned.1.call-update
  79.7 0.0 reduce-scatter.7.cloned.1.call-start
  79.8 0.5 copy-done.6
  80.3 0.1 fusion.9
  80.4 55.4 %reduce-scatter.9.cloned.1.call-done = f32[16,896]{1,0:T(8,128)} async-done(((f32[256,896]{1,0:T(8,128)}), f32[16,896]{1,0:T(8,128)}) %reduce-scatter.9.cloned.1.call-update) | async-done | bytes 57360 | tf_op jit(solution)/shard_map/reduce_scatter | solution.py:88
  135.8 96.3 %reduce-scatter.5.cloned.1.call-done = f32[16,1920]{1,0:T(8,128)} async-done(((f32[256,1920]{1,0:T(8,128)}), f32[16,1920]{1,0:T(8,128)}) %reduce-scatter.5.cloned.1.call-update) | async-done | bytes 122896 | tf_op jit(solution)/shard_map/reduce_scatter | solution.py:54
  232.0 0.0 copy-done.5
  232.0 1.1 multiply_convert_fusion.1
  233.1 43.2 %all_gather.16 = bf16[256,896]{1,0:T(8,128)(2,1)S(1)} all-gather(bf16[16,896]{1,0:T(8,128)(2,1)S(1)} %get-tuple-element.5), channel_id=1, replica_groups=mesh['pipe'=32,'tensor'=16] {'tensor'}, dimensions={0}, use_global_device_ids=true | all-gather | bytes 487424 | tf_op jit(solution)/shard_map/all_gather | solution.py:78
  276.3 1.2 fusion.16
  277.5 0.0 reduce-scatter.7.cloned.1.call-update
  277.6 0.0 reduce-scatter.11.cloned.1.call-start
  277.6 46.3 %all_gather.18 = bf16[256,1792]{1,0:T(8,128)(2,1)S(1)} all-gather(bf16[16,1792]{1,0:T(8,128)(2,1)S(1)} %pad_maximum_fusion.1), channel_id=1, replica_groups=mesh['pipe'=32,'tensor'=16] {'tensor'}, dimensions={0}, use_global_device_ids=true | all-gather | bytes 974848 | tf_op jit(solution)/shard_map/all_gather | solution.py:104
  323.9 0.5 fusion.4
  324.4 1.3 convolution_add_fusion
  325.6 0.0 reduce-scatter.11.cloned.1.call-update
  325.7 0.0 all-reduce.2.cloned.1.call-start
  325.7 0.2 fusion.2
  325.9 54.0 %psum.14 = bf16[16,128]{1,0:T(8,128)(2,1)S(1)} all-reduce(f32[16,128]{1,0:T(8,128)S(1)} %fusion.2), channel_id=1, replica_groups=mesh['pipe'=32,'tensor'=16] {'pipe'}, use_global_device_ids=true, to_apply=%region_5.6 | all-reduce | flops 2048 | bytes 12288 | tf_op jit(solution)/shard_map/psum | solution.py:100
  379.9 40.6 %all_gather.19 = bf16[256,128]{1,0:T(8,128)(2,1)S(1)} all-gather(bf16[16,128]{1,0:T(8,128)(2,1)S(1)} %psum.14), channel_id=1, replica_groups=mesh['pipe'=32,'tensor'=16] {'tensor'}, dimensions={0}, use_global_device_ids=true | all-gather | bytes 69632 | tf_op jit(solution)/shard_map/all_gather | solution.py:101
  420.5 1.8 convolution_multiply_fusion
  422.3 0.0 all-reduce.2.cloned.1.call-update
  422.4 0.9 fusion.18
  423.3 0.0 reduce-scatter.7.cloned.1.call-done
  423.3 1.3 convert_element_type.24
  424.6 87.9 %reduce-scatter.11.cloned.1.call-done = f32[8,512]{1,0:T(8,128)} async-done(((f32[256,512]{1,0:T(8,128)}), f32[8,512]{1,0:T(8,128)}) %reduce-scatter.11.cloned.1.call-update) | async-done | bytes 16400 | tf_op jit(solution)/shard_map/reduce_scatter | solution.py:106
  512.5 1.4 fusion.1
  514.0 165.2 %all-reduce.2.cloned.1.call-done = f32[2,64,896]{2,1,0:T(8,128)} async-done(((f32[2,64,896]{2,1,0:T(8,128)}), f32[2,64,896]{2,1,0:T(8,128)}) %all-reduce.2.cloned.1.call-update) | async-done | bytes 458768 | tf_op jit(solution)/shard_map/psum | solution.py:96
  679.2 1.8 copy.16
  (3 shorter events, 0.0 us)
Async XLA Ops:
  7.2 36.8 %copy-start = (bf16[896,512]{1,0:T(8,128)(2,1)S(1)}, bf16[896,512]{1,0:T(8,128)(2,1)}, u32[]{:S(2)}) copy-start(bf16[896,512]{1,0:T(8,128)(2,1)} %param.11) | copy-start | bytes 2752516
  7.2 38.3 %copy-start.4 = (bf16[8,512]{1,0:T(8,128)(2,1)S(1)}, bf16[8,512]{1,0:T(8,128)(2,1)}, u32[]{:S(2)}) copy-start(bf16[8,512]{1,0:T(8,128)(2,1)} %param.8) | copy-start | bytes 24580
  7.2 69.9 %copy-start.3 = (bf16[2,512,64]{1,2,0:T(8,128)(2,1)S(1)}, bf16[2,512,64]{1,2,0:T(8,128)(2,1)}, u32[]{:S(2)}) copy-start(bf16[2,512,64]{1,2,0:T(8,128)(2,1)} %param.12) | copy-start | bytes 393220
  7.2 128.6 %reduce-scatter.9.cloned.1.call-start = ((), (), s32[]{:S(2)}) async-start(), calls=%async_computation.6 | async-start | bytes 974848 | tf_op jit(solution)/shard_map/reduce_scatter | solution.py:88
  44.0 33.3 %copy-start.1 = (bf16[512,896]{1,0:T(8,128)(2,1)S(1)}, bf16[512,896]{1,0:T(8,128)(2,1)}, u32[]{:S(2)}) copy-start(bf16[512,896]{1,0:T(8,128)(2,1)} %param.9) | copy-start | bytes 2752516
  45.4 32.4 %copy-start.2 = (bf16[512,896]{1,0:T(8,128)(2,1)S(1)}, bf16[512,896]{1,0:T(8,128)(2,1)}, u32[]{:S(2)}) copy-start(bf16[512,896]{1,0:T(8,128)(2,1)} %param.10) | copy-start | bytes 2752516
  45.4 186.6 %reduce-scatter.5.cloned.1.call-start = ((), (), s32[]{:S(2)}) async-start(), calls=%async_computation.4 | async-start | bytes 2088960 | tf_op jit(solution)/shard_map/reduce_scatter | solution.py:54
  79.6 0.7 copy-start.6
  79.6 152.4 %copy-start.5 = (bf16[2,64,896]{2,1,0:T(8,128)(2,1)S(1)}, bf16[2,64,896]{2,1,0:T(8,128)(2,1)}, u32[]{:S(2)}) copy-start(bf16[2,64,896]{2,1,0:T(8,128)(2,1)} %param.13) | copy-start | bytes 688132
  79.7 343.6 %reduce-scatter.7.cloned.1.call-start = ((), (), s32[]{:S(2)}) async-start(), calls=%async_computation.5 | async-start | bytes 540672 | tf_op jit(solution)/shard_map/reduce_scatter | solution.py:80
  277.6 234.9 %reduce-scatter.11.cloned.1.call-start = ((), (), s32[]{:S(2)}) async-start(), calls=%async_computation.7 | async-start | bytes 540672 | tf_op jit(solution)/shard_map/reduce_scatter | solution.py:106
  325.7 353.5 %all-reduce.2.cloned.1.call-start = ((), (), s32[]{:S(2)}) async-start(), calls=%async_computation.8 | async-start | bytes 917504 | tf_op jit(solution)/shard_map/psum | solution.py:96
Sparse Core Ops, SparseCore 0:
  45.5 90.1 reduce-scatter.8
  140.5 91.5 reduce-scatter.4
  277.7 117.5 reduce-scatter.6
  398.1 114.3 reduce-scatter.10
  515.8 163.2 all-reduce.1
where the time goes:
time: 688 us
  waiting for transfers between devices  405 us (59%)
  blocking collectives  252 us (37%)
  between operations  13.9 us (2%)
  matrix products  10.9 us (2%)
    psum x1, waiting for transfers between devices, on_device(): second_factor_gradient = lax.psum(second_factor_term, 'tensor')  165 us
    reduce_scatter x1, waiting for transfers between devices, on_device(): lax.psum_scatter(jnp.concatenate([jnp.dot(piece, gate_weight, preferred_e...  96.3 us
    reduce_scatter x1, waiting for transfers between devices, on_device(): lax.psum_scatter(trailing_product(piece[:, :hidden_shard], gate_weight) +...  87.9 us
    reduce_scatter x1, waiting for transfers between devices, on_device(): lax.psum_scatter(trailing_product(piece, down_weight), 'tensor', scatter_...  55.4 us
    psum x1, blocking collectives, on_device(): low_summed = lax.psum(reduced_gradient, 'pipe')  54 us
    all_gather x1, blocking collectives, on_device(): stacked_all = lax.all_gather(stacked, 'tensor', axis=0, tiled=True)  46.3 us
    all_gather x1, blocking collectives, on_device(): hidden_all = lax.all_gather(hidden, 'tensor', axis=0, tiled=True)  43.2 us
    all_gather x1, blocking collectives, on_device(): low_all = lax.all_gather(low_summed, 'tensor', axis=0, tiled=True)  40.6 us
  transfers between devices with their start and end apart: 5, of which 4 were waited for; matrix products, arithmetic and copies ran while one was open for 1% of the time, Pallas kernels for 0%

commit v1 on v0

--- a/solution.py
+++ b/solution.py
@@ -93,7 +93,7 @@
         jnp.bfloat16
     )
     second_factor_term = adapter_scale * leading_product(reduced_activation, upward_gradient)
-    second_factor_gradient = lax.psum(second_factor_term, "tensor")
+    second_factor_gradient = jnp.sum(lax.all_gather(second_factor_term, "tensor"), axis=0)
     reduced_gradient = (
         adapter_scale * trailing_product(upward_gradient, second_factor_rows) * adapter_select_mask
     )

time: 688 us -> 636 us (0.924)
  the two profiles are of different devices: /device:TPU:2 before, /device:TPU:1 now
where the time goes in v1:
time: 636 us
  waiting for transfers between devices  355 us (56%)
  blocking collectives  249 us (39%)
  between operations  13.9 us (2%)
  matrix products  10.9 us (2%)
  other arithmetic  7.08 us (1%)
    all_gather x1, waiting for transfers between devices, on_device(): lax.all_gather(second_factor_term, 'tensor')  113 us
    reduce_scatter x1, waiting for transfers between devices, on_device(): lax.psum_scatter(jnp.concatenate([jnp.dot(piece, gate_weight, preferred_e...  97.4 us
    reduce_scatter x1, waiting for transfers between devices, on_device(): lax.psum_scatter(trailing_product(piece[:, :hidden_shard], gate_weight) +...  91.9 us
    psum x1, blocking collectives, on_device(): low_summed = lax.psum(reduced_gradient, 'pipe')  66.5 us
    reduce_scatter x1, waiting for transfers between devices, on_device(): lax.psum_scatter(trailing_product(piece, down_weight), 'tensor', scatter_...  51.8 us
    all_gather x1, blocking collectives, on_device(): stacked_all = lax.all_gather(stacked, 'tensor', axis=0, tiled=True)  41.4 us
    all_gather x1, blocking collectives, on_device(): adjoint_rows = lax.all_gather(cotangent, 'pipe', axis=0, tiled=True)  38.2 us
    all_gather x1, blocking collectives, on_device(): hidden_all = lax.all_gather(hidden, 'tensor', axis=0, tiled=True)  37.6 us
  transfers between devices with their start and end apart: 5, of which 4 were waited for; matrix products, arithmetic and copies ran while one was open for 2% of the time, Pallas kernels for 0%

profile of v1, /device:TPU:1, one launch (start us, length us, event | category | flops | bytes accessed | tf_op | source)
XLA Modules:
  0.0 635.7 jit_solution(13800165477685143225)
XLA Ops:
  7.2 0.0 copy-start
  7.2 0.0 copy-start.4
  7.2 0.0 copy-start.3
  7.2 0.0 reduce-scatter.9.cloned.1.call-start
  7.2 38.2 %all_gather.23 = bf16[256,512]{1,0:T(8,128)(2,1)S(1)} all-gather(bf16[8,512]{1,0:T(8,128)(2,1)} %param.15), channel_id=1, replica_groups=mesh['pipe'=32,'tensor'=16] {'pipe'}, dimensions={0}, use_global_device_ids=true | all-gather | bytes 270336 | tf_op jit(solution)/shard_map/all_gather | solution.py:86
  45.5 0.0 copy-done
  45.5 0.0 copy-start.2
  45.5 1.4 fusion.17
  46.9 0.0 copy-start.1
  46.9 0.0 reduce-scatter.9.cloned.1.call-update
  46.9 0.0 reduce-scatter.5.cloned.1.call-start
  47.0 0.0 copy-done.4
  47.0 33.1 %all_gather.21 = bf16[256,512]{1,0:T(8,128)(2,1)S(1)} all-gather(bf16[8,512]{1,0:T(8,128)(2,1)S(1)} %copy-done.4), channel_id=1, replica_groups=mesh['pipe'=32,'tensor'=16] {'pipe'}, dimensions={0}, use_global_device_ids=true | all-gather | bytes 270336 | tf_op jit(solution)/shard_map/all_gather | solution.py:52
  80.1 0.0 copy-done.3
  80.1 0.2 fusion.15
  80.4 0.0 copy-done.2
  80.4 0.4 fusion.14
  80.8 0.0 copy-done.1
  80.8 0.4 fusion.13
  81.3 1.4 pad_maximum_fusion
  82.7 0.0 copy-start.6
  82.7 0.0 copy-start.5
  82.7 0.0 reduce-scatter.5.cloned.1.call-update
  82.7 0.0 reduce-scatter.7.cloned.1.call-start
  82.8 0.5 copy-done.6
  83.4 0.1 fusion.9
  83.4 51.8 %reduce-scatter.9.cloned.1.call-done = f32[16,896]{1,0:T(8,128)} async-done(((f32[256,896]{1,0:T(8,128)}), f32[16,896]{1,0:T(8,128)}) %reduce-scatter.9.cloned.1.call-update) | async-done | bytes 57360 | tf_op jit(solution)/shard_map/reduce_scatter | solution.py:88
  135.3 97.4 %reduce-scatter.5.cloned.1.call-done = f32[16,1920]{1,0:T(8,128)} async-done(((f32[256,1920]{1,0:T(8,128)}), f32[16,1920]{1,0:T(8,128)}) %reduce-scatter.5.cloned.1.call-update) | async-done | bytes 122896 | tf_op jit(solution)/shard_map/reduce_scatter | solution.py:54
  232.7 0.0 copy-done.5
  232.7 1.1 multiply_convert_fusion.1
  233.8 37.6 %all_gather.22 = bf16[256,896]{1,0:T(8,128)(2,1)S(1)} all-gather(bf16[16,896]{1,0:T(8,128)(2,1)S(1)} %get-tuple-element.5), channel_id=1, replica_groups=mesh['pipe'=32,'tensor'=16] {'tensor'}, dimensions={0}, use_global_device_ids=true | all-gather | bytes 487424 | tf_op jit(solution)/shard_map/all_gather | solution.py:78
  271.4 1.2 fusion.16
  272.6 0.0 reduce-scatter.7.cloned.1.call-update
  272.6 0.0 reduce-scatter.11.cloned.1.call-start
  272.7 41.4 %all_gather.24 = bf16[256,1792]{1,0:T(8,128)(2,1)S(1)} all-gather(bf16[16,1792]{1,0:T(8,128)(2,1)S(1)} %pad_maximum_fusion.1), channel_id=1, replica_groups=mesh['pipe'=32,'tensor'=16] {'tensor'}, dimensions={0}, use_global_device_ids=true | all-gather | bytes 974848 | tf_op jit(solution)/shard_map/all_gather | solution.py:104
  314.1 0.5 fusion.4
  314.6 1.3 convolution_add_fusion
  315.9 0.0 reduce-scatter.11.cloned.1.call-update
  315.9 0.0 all-gather.3.cloned.1.call-start
  316.0 1.8 convolution_multiply_fusion
  317.8 0.0 all-gather.3.cloned.1.call-update
  317.8 0.2 fusion.2
  318.0 66.5 %psum.7 = bf16[16,128]{1,0:T(8,128)(2,1)S(1)} all-reduce(f32[16,128]{1,0:T(8,128)S(1)} %fusion.2), channel_id=1, replica_groups=mesh['pipe'=32,'tensor'=16] {'pipe'}, use_global_device_ids=true, to_apply=%region_5.6 | all-reduce | flops 2048 | bytes 12288 | tf_op jit(solution)/shard_map/psum | solution.py:100
  384.5 31.7 %all_gather.25 = bf16[256,128]{1,0:T(8,128)(2,1)S(1)} all-gather(bf16[16,128]{1,0:T(8,128)(2,1)S(1)} %psum.7), channel_id=1, replica_groups=mesh['pipe'=32,'tensor'=16] {'tensor'}, dimensions={0}, use_global_device_ids=true | all-gather | bytes 69632 | tf_op jit(solution)/shard_map/all_gather | solution.py:101
  416.1 0.9 fusion.18
  417.0 0.0 reduce-scatter.7.cloned.1.call-done
  417.0 1.3 convert_element_type.24
  418.4 91.9 %reduce-scatter.11.cloned.1.call-done = f32[8,512]{1,0:T(8,128)} async-done(((f32[256,512]{1,0:T(8,128)}), f32[8,512]{1,0:T(8,128)}) %reduce-scatter.11.cloned.1.call-update) | async-done | bytes 16400 | tf_op jit(solution)/shard_map/reduce_scatter | solution.py:106
  510.3 1.4 fusion.1
  511.7 113.3 %all-gather.3.cloned.1.call-done = f32[2048,896]{1,0:T(8,128)} async-done(((f32[128,896]{1,0:T(8,128)}), f32[2048,896]{1,0:T(8,128)}) %all-gather.3.cloned.1.call-update) | async-done | bytes 7340048 | tf_op jit(solution)/shard_map/all_gather | solution.py:96
  625.0 4.2 reduce_sum.19
  (3 shorter events, 0.0 us)
Async XLA Ops:
  7.2 38.3 %copy-start = (bf16[896,512]{1,0:T(8,128)(2,1)S(1)}, bf16[896,512]{1,0:T(8,128)(2,1)}, u32[]{:S(2)}) copy-start(bf16[896,512]{1,0:T(8,128)(2,1)} %param.11) | copy-start | bytes 2752516
  7.2 39.8 %copy-start.4 = (bf16[8,512]{1,0:T(8,128)(2,1)S(1)}, bf16[8,512]{1,0:T(8,128)(2,1)}, u32[]{:S(2)}) copy-start(bf16[8,512]{1,0:T(8,128)(2,1)} %param.8) | copy-start | bytes 24580
  7.2 72.9 %copy-start.3 = (bf16[2,512,64]{1,2,0:T(8,128)(2,1)S(1)}, bf16[2,512,64]{1,2,0:T(8,128)(2,1)}, u32[]{:S(2)}) copy-start(bf16[2,512,64]{1,2,0:T(8,128)(2,1)} %param.12) | copy-start | bytes 393220
  7.2 128.1 %reduce-scatter.9.cloned.1.call-start = ((), (), s32[]{:S(2)}) async-start(), calls=%async_computation.6 | async-start | bytes 974848 | tf_op jit(solution)/shard_map/reduce_scatter | solution.py:88
  45.5 34.9 %copy-start.2 = (bf16[512,896]{1,0:T(8,128)(2,1)S(1)}, bf16[512,896]{1,0:T(8,128)(2,1)}, u32[]{:S(2)}) copy-start(bf16[512,896]{1,0:T(8,128)(2,1)} %param.10) | copy-start | bytes 2752516
  46.9 33.9 %copy-start.1 = (bf16[512,896]{1,0:T(8,128)(2,1)S(1)}, bf16[512,896]{1,0:T(8,128)(2,1)}, u32[]{:S(2)}) copy-start(bf16[512,896]{1,0:T(8,128)(2,1)} %param.9) | copy-start | bytes 2752516
  46.9 185.7 %reduce-scatter.5.cloned.1.call-start = ((), (), s32[]{:S(2)}) async-start(), calls=%async_computation.4 | async-start | bytes 2088960 | tf_op jit(solution)/shard_map/reduce_scatter | solution.py:54
  82.7 0.7 copy-start.6
  82.7 150.0 %copy-start.5 = (bf16[2,64,896]{2,1,0:T(8,128)(2,1)S(1)}, bf16[2,64,896]{2,1,0:T(8,128)(2,1)}, u32[]{:S(2)}) copy-start(bf16[2,64,896]{2,1,0:T(8,128)(2,1)} %param.13) | copy-start | bytes 688132
  82.7 334.3 %reduce-scatter.7.cloned.1.call-start = ((), (), s32[]{:S(2)}) async-start(), calls=%async_computation.5 | async-start | bytes 540672 | tf_op jit(solution)/shard_map/reduce_scatter | solution.py:80
  272.6 237.6 %reduce-scatter.11.cloned.1.call-start = ((), (), s32[]{:S(2)}) async-start(), calls=%async_computation.7 | async-start | bytes 540672 | tf_op jit(solution)/shard_map/reduce_scatter | solution.py:106
  315.9 309.0 %all-gather.3.cloned.1.call-start = ((), (), s32[]{:S(2)}) async-start(), calls=%async_computation.8 | async-start | bytes 7798784 | tf_op jit(solution)/shard_map/all_gather | solution.py:96
Sparse Core Ops, SparseCore 0:
  47.1 88.1 reduce-scatter.8
  140.0 92.6 reduce-scatter.4
  272.8 121.1 reduce-scatter.6
  396.8 113.4 reduce-scatter.10
  513.7 111.2 all-gather.2
